TPU v7x, 32 devices: a whole 2x2x4 slice. The times are simulated.
32 devices in a mesh: ctx: 8 (over y, x, core), fsdp: 4 (over z).
Axes of the slice: x: 2, y: 2, z: 4, core: 2. Of those that a mesh axis runs over, the one named last changes fastest.
Arguments:
- loaded: bfloat16 [8, 8, 128, 4096], P('ctx', None, None, 'fsdp'), may hold values from -6 to 6
- slot_pos: int32 [8, 8, 128], P('ctx'), may hold values from -1 to 255, as said below
- contig_lengths: int32 [16], replicated, may hold values from 1 to 1024, 2048 in all
- w_in: bfloat16 [4096, 3, 4096], P('ctx', None, 'fsdp'), may hold values from -0.09375 to 0.09375
- short_taps: float32 [3, 7, 4096], P(None, None, 'fsdp'), may hold values from -2 to 2
- long_taps: float32 [128, 4096], P(None, 'fsdp'), may hold values from -0.5 to 0.5
- grad_out: bfloat16 [2048, 4096], P('ctx', 'fsdp'), may hold values from -0.59765625 to 0.59765625
Outputs:
- gated_out: bfloat16 [2048, 4096], P('ctx', 'fsdp')
- token_grads: bfloat16 [2048, 4096], P('ctx', 'fsdp')
- weight_grads: bfloat16 [4096, 3, 4096], P('ctx', None, 'fsdp')
- short_grads: float32 [3, 7, 4096], P(None, None, 'fsdp')
- long_grads: float32 [128, 4096], P(None, 'fsdp')
Inputs may be any that keep to these rules, and one draw needn't show every extreme that they name: `slot_pos`: for each destination e, the slots with a value of 0 or more name every row 0 to 255 of e's block exactly once; -1 marks an empty slot; for each destination some loader fills all 128 of its slots. `contig_lengths`: the lengths sum to 2048.
All inputs are finite; a program needn't handle non-finite values.
Results may differ from a plain program's by a relative error of at most 0.012.
Values may be sent and summed in bfloat16 or wider, within the bound.
A program may use at most 192 MiB of HBM per device.

v0:
```python
import jax
import jax.numpy as jnp
from jax import lax
from jax.sharding import PartitionSpec as P


def passed_along(x, axis, by):
    size = lax.axis_size(axis)
    pairs = [(i, i + by) for i in range(size) if 0 <= i + by < size]
    return lax.ppermute(x, axis, pairs)


def starts_of(positions, contig_lengths):
    ends = jnp.cumsum(contig_lengths, dtype=jnp.int32)
    begins = ends - contig_lengths
    chosen = jnp.where(begins[None, :] <= positions[:, None], begins[None, :], 0)
    return jnp.max(chosen, axis=1)


def lead_filter(ext, taps, positions, begins_here):
    width = taps.shape[0]
    count = ext.shape[0] - width + 1
    bcast_shape = (count,) + (1,) * (ext.ndim - 1)
    total = jnp.zeros((count,) + ext.shape[1:], jnp.float32)
    for tap_index in range(width):
        keep_mask = (positions - tap_index >= begins_here).astype(jnp.float32).reshape(bcast_shape)
        first = width - 1 - tap_index
        total = total + taps[tap_index] * ext[first : first + count] * keep_mask
    return total


def trail_filter(ext, taps, positions, begins_ext):
    width = taps.shape[0]
    count = ext.shape[0] - width + 1
    bcast_shape = (count,) + (1,) * (ext.ndim - 1)
    total = jnp.zeros((count,) + ext.shape[1:], jnp.float32)
    for tap_index in range(width):
        keep_mask = (
            (positions >= begins_ext[tap_index : tap_index + count])
            .astype(jnp.float32)
            .reshape(bcast_shape)
        )
        total = total + taps[tap_index] * ext[tap_index : tap_index + count] * keep_mask
    return total


def tap_sums(grads, ext, width, lead_count, positions, begins_here):
    count = grads.shape[0]
    bcast_shape = (count,) + (1,) * (grads.ndim - 1)
    pieces = []
    for tap_index in range(width):
        keep_mask = (positions - tap_index >= begins_here).astype(jnp.float32).reshape(bcast_shape)
        first = lead_count - tap_index
        pieces.append(jnp.sum(grads * ext[first : first + count] * keep_mask, axis=0))
    return jnp.stack(pieces, 0)


def on_device(loaded, slot_pos, contig_lengths, w_in, short_taps, long_taps, grad_out):
    moved = lax.all_to_all(loaded, "ctx", split_axis=1, concat_axis=0, tiled=True)
    feat_cols = moved.shape[3]
    slot_rows = moved.reshape(-1, feat_cols)
    tok_rows = grad_out.shape[0]
    short_width = short_taps.shape[1]
    long_width = long_taps.shape[0]
    targets = slot_pos.reshape(-1)
    picker = (targets[None, :] == jnp.arange(tok_rows, dtype=jnp.int32)[:, None]).astype(
        jnp.bfloat16
    )
    own_part = jnp.dot(picker, slot_rows, preferred_element_type=jnp.float32).astype(jnp.bfloat16)
    tokens = lax.all_gather(own_part, "fsdp", axis=1, tiled=True)
    gathered = lax.all_gather(w_in, "ctx", axis=0, tiled=True)
    streams = jnp.einsum("td,dsc->tsc", tokens, gathered, preferred_element_type=jnp.float32)
    proj_half = streams.astype(jnp.bfloat16)
    offset = lax.axis_index("ctx") * tok_rows
    positions = offset + jnp.arange(tok_rows, dtype=jnp.int32)
    begins_here = starts_of(positions, contig_lengths)
    short_lags = jnp.transpose(short_taps, (1, 0, 2))
    prev_rows = passed_along(proj_half[tok_rows - (short_width - 1) :], "ctx", 1)
    lead_mixed = jnp.concatenate([prev_rows, proj_half], 0).astype(jnp.float32)
    lead_count = short_width - 1
    filtered = lead_filter(lead_mixed, short_lags, positions, begins_here)
    product = (filtered[:, 1] * filtered[:, 2]).astype(jnp.bfloat16)
    prior_rows = passed_along(product[tok_rows - (long_width - 1) :], "ctx", 1)
    lead_product = jnp.concatenate([prior_rows, product], 0).astype(jnp.float32)
    carried = lead_filter(lead_product, long_taps, positions, begins_here)
    gated_out = (filtered[:, 0] * carried).astype(jnp.bfloat16)
    upstream = grad_out.astype(jnp.float32)
    back_prod = (upstream * filtered[:, 0]).astype(jnp.bfloat16)
    first_grad = upstream * carried
    next_rows = passed_along(back_prod[: long_width - 1], "ctx", -1)
    long_begins = starts_of(
        offset + jnp.arange(tok_rows + long_width - 1, dtype=jnp.int32), contig_lengths
    )
    trail_prod = jnp.concatenate([back_prod, next_rows], 0).astype(jnp.float32)
    grad_product = trail_filter(trail_prod, long_taps, positions, long_begins)
    grad_filtered = jnp.stack(
        [first_grad, grad_product * filtered[:, 2], grad_product * filtered[:, 1]], 1
    ).astype(jnp.bfloat16)
    next_grads = passed_along(grad_filtered[: short_width - 1], "ctx", -1)
    short_begins = starts_of(
        offset + jnp.arange(tok_rows + short_width - 1, dtype=jnp.int32), contig_lengths
    )
    trail_grad = jnp.concatenate([grad_filtered, next_grads], 0).astype(jnp.float32)
    grad_mixed = trail_filter(trail_grad, short_lags, positions, short_begins).astype(jnp.bfloat16)
    long_local = tap_sums(
        back_prod.astype(jnp.float32),
        lead_product,
        long_width,
        long_width - 1,
        positions,
        begins_here,
    )
    short_local = tap_sums(
        grad_filtered.astype(jnp.float32),
        lead_mixed,
        short_width,
        lead_count,
        positions,
        begins_here,
    )
    short_total, long_total = (
        lax.psum(jnp.transpose(short_local, (1, 0, 2)).astype(jnp.bfloat16), "ctx").astype(
            jnp.float32
        ),
        lax.psum(long_local.astype(jnp.bfloat16), "ctx").astype(jnp.float32),
    )
    partial_value = jnp.einsum(
        "tsc,dsc->td", grad_mixed, gathered, preferred_element_type=jnp.float32
    )
    token_grads = lax.psum_scatter(
        partial_value.astype(jnp.bfloat16), "fsdp", scatter_dimension=1, tiled=True
    )
    weight_grads = lax.psum_scatter(
        jnp.einsum("td,tsc->dsc", tokens, grad_mixed, preferred_element_type=jnp.float32).astype(
            jnp.bfloat16
        ),
        "ctx",
        scatter_dimension=0,
        tiled=True,
    )
    return (gated_out, token_grads, weight_grads, short_total, long_total)


def solution(mesh):
    in_specs = (
        P("ctx", None, None, "fsdp"),
        P("ctx", None, None),
        P(),
        P("ctx", None, "fsdp"),
        P(None, None, "fsdp"),
        P(None, "fsdp"),
        P("ctx", "fsdp"),
    )
    out_specs = (
        P("ctx", "fsdp"),
        P("ctx", "fsdp"),
        P("ctx", None, "fsdp"),
        P(None, None, "fsdp"),
        P(None, "fsdp"),
    )
    return jax.shard_map(
        on_device, mesh=mesh, in_specs=in_specs, out_specs=out_specs, check_vma=False
    )
```

profile of v0, /device:TPU:0, one launch (start us, length us, event | category | flops | bytes accessed | tf_op | source)
XLA Modules:
  0.0 702.3 jit_solution(11985297371757299991)
XLA Ops:
  7.2 31.8 %all_to_all.4 = bf16[1,8,128,1024]{3,2,0,1:T(8,128)(2,1)S(1)} all-to-all(bf16[1,8,128,1024]{3,2,0,1:T(8,128)(2,1)} %bitcast.209), channel_id=1, replica_groups=mesh['ctx'=8,'fsdp'=4] {'ctx'}, dimensions={1} | all-to-all | bytes 4194304 | tf_op jit(solution)/shard_map/all_to_all | solution.py:59
  53.0 33.0 %all-gather.3.cloned.1.call-done = bf16[256,4096]{1,0:T(8,128)(2,1)} async-done(((bf16[256,1024]{1,0:T(8,128)(2,1)}), bf16[256,4096]{1,0:T(8,128)(2,1)}) %all-gather.3.cloned.1.call-update) | async-done | bytes 2097168 | tf_op jit(solution)/shard_map/all_gather | solution.py:70
  86.0 126.0 %all-gather.5.cloned.1.call-done = bf16[4096,3,1024]{2,0,1:T(8,128)(2,1)} async-done(((bf16[512,3,1024]{2,0,1:T(8,128)(2,1)}), bf16[4096,3,1024]{2,0,1:T(8,128)(2,1)}) %all-gather.5.cloned.1.call-update) | async-done | bytes 25165840 | tf_op jit(solution)/shard_map/all_gather | solution.py:71
  212.0 12.2 %fusion.32 = bf16[256,3,1024]{2,0,1:T(8,128)(2,1)S(1)} fusion(bf16[4096,3,1024]{2,0,1:T(8,128)(2,1)} %all-gather.5.cloned.1.call-done, bf16[256,4096]{1,0:T(8,128)(2,1)} %all-gather.3.cloned.1.call-done), kind=kOutput, calls=%fused_computation.177 | convolution fusion | flops 6443237376 | bytes 28835840 | tf_op jit(solution)/shard_map/td,dsc->tsc/dot_general | solution.py:72
  227.8 3.6 multiply_add_fusion
  231.7 3.7 collective-permute-start.1
  237.0 3.4 fusion.266
  242.6 3.3 fusion.268
  245.9 3.3 fusion.270
  249.2 3.3 fusion.272
  252.5 3.3 fusion.274
  258.9 3.3 fusion.278
  262.1 3.3 fusion.280
  265.4 3.3 fusion.282
  268.8 3.3 fusion.284
  272.1 3.3 fusion.286
  275.5 3.5 fusion.288
  279.3 3.3 fusion.290
  283.0 9.1 %multiply_add_fusion.2 = f32[256,1024]{1,0:T(8,128)S(1)} fusion(f32[383,1024]{1,0:T(8,128)S(1)} %maximum_convert_fusion.2, f32[256]{0:T(256)} %copy-done.108, f32[1024]{0:T(1024)S(1)} %bitcast.309, f32[256]{0:T(256)} %copy-done.109, f32[1024]{0:T(1024)S(1)} %bitcast.312, f32[256]{0:T(256)} %copy-done.110, f32[1024]{0:T(1024)S(1)} %bitcast.314, ...), kind=kLoop, calls=%fused_computation.832 | loop fusion | flops 33554432 | bytes 46357504 | tf_op jit(solution)/shard_map/add | solution.py:28
  292.1 19.1 %fusion.550 = (bf16[256,1,1024]{2,0,1:T(8,128)(2,1)}, f32[256,1024]{1,0:T(8,128)}) fusion(bf16[256,1024]{1,0:T(8,128)(2,1)} %param.13, f32[256]{0:T(256)} %get-tuple-element.435, f32[383,1024]{1,0:T(8,128)S(1)} %maximum_convert_fusion.2, f32[1024]{0:T(1024)} %bitcast.279, f32[256]{0:T(256)} %get-tuple-element.436, f32[1024]{0:T(1024)} %bitcast.281, ...), kind=kLoop, calls=%fused_computation.840 | loop fusion | flops 67633152 | bytes 92709888 | tf_op jit(solution)/shard_map/stack | solution.py:96
  316.3 8.4 %fusion.486 = f32[256,1024]{1,0:T(8,128)} fusion(f32[383,1024]{1,0:T(8,128)S(1)} %maximum_convert_fusion.3, f32[256]{0:T(256)} %get-tuple-element.407, f32[256]{0:T(256)} %get-tuple-element.408, f32[256]{0:T(256)} %get-tuple-element.409, f32[256]{0:T(256)} %get-tuple-element.410, f32[256]{0:T(256)} %get-tuple-element.411, f32[256]{0:T(256)} %get-tuple-element.412, ...), kind=kLoop, calls=%fused_computation.732 | loop fusion | flops 24903680 | bytes 34766848 | tf_op jit(solution)/shard_map/add | solution.py:43
  324.8 25.0 %fusion.548 = (bf16[256,1,1024]{2,0,1:T(8,128)(2,1)}, f32[256,1024]{1,0:T(8,128)}) fusion(f32[256,3,1024]{2,0,1:T(8,128)} %copy-done.4, f32[256]{0:T(256)} %get-tuple-element.307, f32[383,1024]{1,0:T(8,128)S(1)} %maximum_convert_fusion.3, f32[1024]{0:T(1024)S(1)} %bitcast.280, f32[256]{0:T(256)} %get-tuple-element.308, f32[1024]{0:T(1024)S(1)} %bitcast.282, ...), kind=kLoop, calls=%fused_computation.838 | loop fusion | flops 76021760 | bytes 104824832 | tf_op jit(solution)/shard_map/stack | solution.py:96
  349.9 3.4 fusion.549
  416.0 10.6 %stack.704 = bf16[128,1024]{1,0:T(8,128)(2,1)} concatenate(bf16[1,1024]{1,0:T(2,128)(2,1)S(1)} %stack.576, bf16[1,1024]{1,0:T(2,128)(2,1)S(1)} %stack.577, bf16[1,1024]{1,0:T(2,128)(2,1)S(1)} %stack.578, bf16[1,1024]{1,0:T(2,128)(2,1)S(1)} %stack.579, bf16[1,1024]{1,0:T(2,128)(2,1)S(1)} %stack.580, bf16[1,1024]{1,0:T(2,128)(2,1)S(1)} %stack.581, bf16[1,1024]{1,0:T(2,128)(2,1)S(1)} %stack.582, ...), dimensions={0} | concatenate | bytes 524288 | tf_op jit(solution)/shard_map/stack | solution.py:55
  427.2 3.9 fusion.17
  431.0 13.2 %fusion = bf16[256,4096]{1,0:T(8,128)(2,1)} fusion(bf16[256,3,1024]{2,0,1:T(8,128)(2,1)S(1)} %fusion.17, bf16[4096,3,1024]{2,0,1:T(8,128)(2,1)} %all-gather.5.cloned.1.call-done), kind=kOutput, calls=%fused_computation.137 | convolution fusion | flops 6443499520 | bytes 28835840 | tf_op jit(solution)/shard_map/tsc,dsc->td/dot_general | solution.py:127
  444.3 13.5 %convolution_convert_fusion = bf16[4096,3,1024]{2,0,1:T(8,128)(2,1)} fusion(bf16[256,3,1024]{2,0,1:T(8,128)(2,1)S(1)} %fusion.17, bf16[256,4096]{1,0:T(8,128)(2,1)} %all-gather.3.cloned.1.call-done), kind=kOutput, calls=%fused_computation.128 | convolution fusion | flops 6455033856 | bytes 28835840 | tf_op jit(solution)/shard_map/td,tsc->dsc/dot_general | solution.py:134
  457.8 31.4 %all-reduce.2.cloned.1.call-done = bf16[128,1024]{1,0:T(8,128)(2,1)} async-done(((bf16[128,1024]{1,0:T(8,128)(2,1)}), bf16[128,1024]{1,0:T(8,128)(2,1)}) %all-reduce.2.cloned.1.call-update) | async-done | bytes 262160 | tf_op jit(solution)/shard_map/psum | solution.py:125
  493.3 3.7 fusion.14
  497.1 23.5 %psum.14 = bf16[3,7,1024]{2,0,1:T(4,128)(2,1)S(1)} all-reduce(bf16[3,7,1024]{2,0,1:T(4,128)(2,1)S(1)} %bitcast.214), channel_id=1, replica_groups=mesh['ctx'=8,'fsdp'=4] {'ctx'}, use_global_device_ids=true, to_apply=%region_13.14 | all-reduce | flops 21504 | bytes 86016 | tf_op jit(solution)/shard_map/psum | solution.py:122
  521.3 14.0 %reduce-scatter.3.cloned.1.call-done = bf16[256,1024]{1,0:T(8,128)(2,1)} async-done(((bf16[256,4096]{1,0:T(8,128)(2,1)}), bf16[256,1024]{1,0:T(8,128)(2,1)}) %reduce-scatter.3.cloned.1.call-update) | async-done | bytes 524304 | tf_op jit(solution)/shard_map/reduce_scatter | solution.py:130
  535.3 160.2 %reduce-scatter.5.cloned.1.call-done = bf16[512,3,1024]{2,0,1:T(8,128)(2,1)} async-done(((bf16[4096,3,1024]{2,0,1:T(8,128)(2,1)}), bf16[512,3,1024]{2,0,1:T(8,128)(2,1)}) %reduce-scatter.5.cloned.1.call-update) | async-done | bytes 3145744 | tf_op jit(solution)/shard_map/reduce_scatter | solution.py:133
  (571 shorter events, 96.0 us)
Async XLA Ops:
  7.2 78.8 %all-gather.3.cloned.1.call-start = ((), (), s32[]{:S(2)}) async-start(), calls=%async_computation.3 | async-start | bytes 2621440 | tf_op jit(solution)/shard_map/all_gather | solution.py:70
  40.6 171.5 %all-gather.5.cloned.1.call-start = ((), (), s32[]{:S(2)}) async-start(), calls=%async_computation.4 | async-start | bytes 28311552 | tf_op jit(solution)/shard_map/all_gather | solution.py:71
  41.3 447.9 %all-reduce.2.cloned.1.call-start = ((), (), s32[]{:S(2)}) async-start(), calls=%async_computation.7 | async-start | bytes 524288 | tf_op jit(solution)/shard_map/psum | solution.py:125
  52.8 216.0 %copy-start.110 = (f32[256]{0:T(256)}, f32[256]{0:T(256)S(1)}, u32[]{:S(2)}) copy-start(f32[256]{0:T(256)S(1)} %get-tuple-element.521) | copy-start | bytes 3076
  52.8 215.9 %copy-start.111 = (f32[256]{0:T(256)}, f32[256]{0:T(256)S(1)}, u32[]{:S(2)}) copy-start(f32[256]{0:T(256)S(1)} %get-tuple-element.522) | copy-start | bytes 3076
  52.8 215.9 %copy-start.112 = (f32[256]{0:T(256)}, f32[256]{0:T(256)S(1)}, u32[]{:S(2)}) copy-start(f32[256]{0:T(256)S(1)} %get-tuple-element.523) | copy-start | bytes 3076
  52.8 215.9 %copy-start.113 = (f32[256]{0:T(256)}, f32[256]{0:T(256)S(1)}, u32[]{:S(2)}) copy-start(f32[256]{0:T(256)S(1)} %get-tuple-element.524) | copy-start | bytes 3076
  52.8 219.2 %copy-start.118 = (f32[256]{0:T(256)}, f32[256]{0:T(256)S(1)}, u32[]{:S(2)}) copy-start(f32[256]{0:T(256)S(1)} %get-tuple-element.529) | copy-start | bytes 3076
  52.8 219.2 %copy-start.119 = (f32[256]{0:T(256)}, f32[256]{0:T(256)S(1)}, u32[]{:S(2)}) copy-start(f32[256]{0:T(256)S(1)} %get-tuple-element.530) | copy-start | bytes 3076
  52.9 219.2 %copy-start.120 = (f32[256]{0:T(256)}, f32[256]{0:T(256)S(1)}, u32[]{:S(2)}) copy-start(f32[256]{0:T(256)S(1)} %get-tuple-element.531) | copy-start | bytes 3076
  52.9 219.2 %copy-start.121 = (f32[256]{0:T(256)}, f32[256]{0:T(256)S(1)}, u32[]{:S(2)}) copy-start(f32[256]{0:T(256)S(1)} %get-tuple-element.532) | copy-start | bytes 3076
  52.9 219.2 %copy-start.122 = (f32[256]{0:T(256)}, f32[256]{0:T(256)S(1)}, u32[]{:S(2)}) copy-start(f32[256]{0:T(256)S(1)} %get-tuple-element.533) | copy-start | bytes 3076
  52.9 219.2 %copy-start.123 = (f32[256]{0:T(256)}, f32[256]{0:T(256)S(1)}, u32[]{:S(2)}) copy-start(f32[256]{0:T(256)S(1)} %get-tuple-element.534) | copy-start | bytes 3076
  52.9 219.2 %copy-start.124 = (f32[256]{0:T(256)}, f32[256]{0:T(256)S(1)}, u32[]{:S(2)}) copy-start(f32[256]{0:T(256)S(1)} %get-tuple-element.535) | copy-start | bytes 3076
  52.9 219.2 %copy-start.125 = (f32[256]{0:T(256)}, f32[256]{0:T(256)S(1)}, u32[]{:S(2)}) copy-start(f32[256]{0:T(256)S(1)} %get-tuple-element.536) | copy-start | bytes 3076
  52.9 222.5 %copy-start.126 = (f32[256]{0:T(256)}, f32[256]{0:T(256)S(1)}, u32[]{:S(2)}) copy-start(f32[256]{0:T(256)S(1)} %get-tuple-element.537) | copy-start | bytes 3076
  52.9 222.5 %copy-start.127 = (f32[256]{0:T(256)}, f32[256]{0:T(256)S(1)}, u32[]{:S(2)}) copy-start(f32[256]{0:T(256)S(1)} %get-tuple-element.538) | copy-start | bytes 3076
  52.9 222.5 %copy-start.128 = (f32[256]{0:T(256)}, f32[256]{0:T(256)S(1)}, u32[]{:S(2)}) copy-start(f32[256]{0:T(256)S(1)} %get-tuple-element.539) | copy-start | bytes 3076
  52.9 222.5 %copy-start.129 = (f32[256]{0:T(256)}, f32[256]{0:T(256)S(1)}, u32[]{:S(2)}) copy-start(f32[256]{0:T(256)S(1)} %get-tuple-element.540) | copy-start | bytes 3076
  53.0 222.5 %copy-start.130 = (f32[256]{0:T(256)}, f32[256]{0:T(256)S(1)}, u32[]{:S(2)}) copy-start(f32[256]{0:T(256)S(1)} %get-tuple-element.541) | copy-start | bytes 3076
  53.0 222.5 %copy-start.131 = (f32[256]{0:T(256)}, f32[256]{0:T(256)S(1)}, u32[]{:S(2)}) copy-start(f32[256]{0:T(256)S(1)} %get-tuple-element.542) | copy-start | bytes 3076
  53.0 222.5 %copy-start.132 = (f32[256]{0:T(256)}, f32[256]{0:T(256)S(1)}, u32[]{:S(2)}) copy-start(f32[256]{0:T(256)S(1)} %get-tuple-element.543) | copy-start | bytes 3076
  53.0 222.5 %copy-start.133 = (f32[256]{0:T(256)}, f32[256]{0:T(256)S(1)}, u32[]{:S(2)}) copy-start(f32[256]{0:T(256)S(1)} %get-tuple-element.544) | copy-start | bytes 3076
  53.0 225.9 %copy-start.134 = (f32[256]{0:T(256)}, f32[256]{0:T(256)S(1)}, u32[]{:S(2)}) copy-start(f32[256]{0:T(256)S(1)} %get-tuple-element.545) | copy-start | bytes 3076
  53.0 225.9 %copy-start.135 = (f32[256]{0:T(256)}, f32[256]{0:T(256)S(1)}, u32[]{:S(2)}) copy-start(f32[256]{0:T(256)S(1)} %get-tuple-element.546) | copy-start | bytes 3076
  53.0 225.9 %copy-start.136 = (f32[256]{0:T(256)}, f32[256]{0:T(256)S(1)}, u32[]{:S(2)}) copy-start(f32[256]{0:T(256)S(1)} %get-tuple-element.547) | copy-start | bytes 3076
  224.2 3.0 collective-permute-start
  231.7 5.0 collective-permute-start.1
  241.2 73.5 %collective-permute-start.2 = (bf16[127,1024]{1,0:T(8,128)(2,1)}, bf16[127,1024]{1,0:T(8,128)(2,1)S(1)}, u32[]{:S(2)}, u32[]{:S(2)}) collective-permute-start(bf16[127,1024]{1,0:T(8,128)(2,1)} %slice.2608), channel_id=1, source_target_pairs={{4,0},{8,4},{12,8},{16,12},{20,16},{24,20},{28,24},{5,1},{9,5},{13... | collective-permute-start | bytes 780296 | tf_op jit(solution)/shard_map/ppermute | solution.py:10
  353.9 72.8 %collective-permute-start.3 = (bf16[6,3,1024]{2,0,1:T(8,128)(2,1)S(1)}, bf16[6,3,1024]{2,0,1:T(8,128)(2,1)S(1)}, u32[]{:S(2)}, u32[]{:S(2)}) collective-permute-start(bf16[6,3,1024]{2,0,1:T(8,128)(2,1)S(1)} %slice.2737), channel_id=1, source_target_pairs={{4,0},{8,4},{12,8},{16,12},{20,16},{24,20},{28,24},{5,1},{9,5},{13... | collective-permute-start | bytes 110600 | tf_op jit(solution)/shard_map/ppermute | solution.py:10
  426.6 108.7 %reduce-scatter.3.cloned.1.call-start = ((), (), s32[]{:S(2)}) async-start(), calls=%async_computation.5 | async-start | bytes 2621440 | tf_op jit(solution)/shard_map/reduce_scatter | solution.py:130
  444.2 251.3 %reduce-scatter.5.cloned.1.call-start = ((), (), s32[]{:S(2)}) async-start(), calls=%async_computation.6 | async-start | bytes 28311552 | tf_op jit(solution)/shard_map/reduce_scatter | solution.py:133
  (162 other events, 5792.6 us)
Sparse Core Ops, SparseCore 0:
  40.7 45.3 all-gather.2
  87.9 124.0 all-gather.4
  426.8 62.3 all-reduce.1
  492.0 43.2 reduce-scatter.2
  539.4 156.1 reduce-scatter.4
where the time goes:
time: 712 us; the launch traced here: 702 us
  waiting for transfers between devices  366 us (51%)
  other arithmetic  137 us (19%)
  local copies, waits for them, and re-layouts  77.5 us (11%)
  blocking collectives  55.3 us (8%)
  matrix products  40.3 us (6%)
  between operations  17.3 us (2%)
  starting transfers between devices  8.79 us (1%)
    reduce_scatter x1, waiting for transfers between devices, on_device(): lax.psum_scatter(jnp.einsum('td,tsc->dsc', tokens, grad_mixed, preferred_...  160 us
    all_gather x1, waiting for transfers between devices, on_device(): gathered = lax.all_gather(w_in, 'ctx', axis=0, tiled=True)  126 us
    another operation x130, local copies, waits for them, and re-layouts, tap_sums(): return jnp.stack(pieces, 0)  70.2 us
    reduce_sum x17, other arithmetic, tap_sums(): pieces.append(jnp.sum(grads * ext[first:first + count] * keep_mask, axis=0))  52.3 us
    another operation x4, other arithmetic, on_device(): jnp.stack([first_grad, grad_product * filtered[:, 2], grad_product * filt...  47.6 us
    all_gather x1, waiting for transfers between devices, on_device(): tokens = lax.all_gather(own_part, 'fsdp', axis=1, tiled=True)  33 us
    all_to_all x1, blocking collectives, on_device(): lax.all_to_all(loaded, 'ctx', split_axis=1, concat_axis=0, tiled=True)  31.8 us
    psum x1, waiting for transfers between devices, on_device(): lax.psum(long_local.astype(jnp.bfloat16), 'ctx').astype(jnp.float32)  31.4 us
  transfers between devices with their start and end apart: 9, of which 6 were waited for; matrix products, arithmetic and copies ran while one was open for 28% of the time, Pallas kernels for 0%

commit v1 on v0

--- a/solution.py
+++ b/solution.py
@@ -67,7 +67,16 @@
         jnp.bfloat16
     )
     own_part = jnp.dot(picker, slot_rows, preferred_element_type=jnp.float32).astype(jnp.bfloat16)
-    tokens = lax.all_gather(own_part, "fsdp", axis=1, tiled=True)
+    ways = lax.axis_size("fsdp")
+    up = [(d, (d + 1) % ways) for d in range(ways)]
+    down = [(d, (d - 1) % ways) for d in range(ways)]
+    earlier, later = ([own_part], [own_part])
+    for _ in range(ways // 2):
+        earlier.append(lax.ppermute(earlier[-1], "fsdp", up))
+    for _ in range((ways - 1) // 2):
+        later.append(lax.ppermute(later[-1], "fsdp", down))
+    line = jnp.concatenate([*earlier[::-1], *later[1:]], axis=1)
+    tokens = jnp.roll(line, (lax.axis_index("fsdp") - ways // 2) * own_part.shape[1], axis=1)
     gathered = lax.all_gather(w_in, "ctx", axis=0, tiled=True)
     streams = jnp.einsum("td,dsc->tsc", tokens, gathered, preferred_element_type=jnp.float32)
     proj_half = streams.astype(jnp.bfloat16)

time: 712 us -> 644 us (0.904)
  waiting for transfers between devices: 366 us -> 320 us
  blocking collectives: 55.3 us -> 23.7 us
  starting transfers between devices: 8.79 us -> 19.6 us
  other arithmetic: 137 us -> 129 us
    all_gather x1, waiting for transfers between devices: 126 us -> 57.9 us  [on_device(): gathered = lax.all_gather(w_in, 'ctx', axis=0, tiled=True)]
    all_gather x1 -> x0, waiting for transfers between devices: 33 us -> none  [on_device(): tokens = lax.all_gather(own_part, 'fsdp', axis=1, tiled=True)]
    all_to_all x0 -> x1, waiting for transfers between devices: none -> 32 us  [on_device(): lax.all_to_all(loaded, 'ctx', split_axis=1, concat_axis=0, tiled=True)]
    all_to_all x1 -> x0, blocking collectives: 31.8 us -> none  [on_device(): lax.all_to_all(loaded, 'ctx', split_axis=1, concat_axis=0, tiled=True)]
    ppermute x0 -> x3, waiting for transfers between devices: none -> 23.2 us  [the longest x2 20.1 us: on_device(): earlier.append(lax.ppermute(earlier[-1], 'fsdp', up))]
    reduce_sum x17, other arithmetic: 52.3 us -> 44.6 us  [tap_sums(): pieces.append(jnp.sum(grads * ext[first:first + count] * keep_mask, axis=0))]
  transfers between devices with their start and end apart: 9 -> 12, of which waited for: 6 -> 9; matrix products, arithmetic and copies ran while one was open for 28% -> 31% of each run, Pallas kernels for 0% -> 0%
where the time goes in v1:
time: 644 us; the launch traced here: 634 us
  waiting for transfers between devices  320 us (50%)
  other arithmetic  129 us (20%)
  local copies, waits for them, and re-layouts  84.4 us (13%)
  matrix products  39.5 us (6%)
  blocking collectives  23.7 us (4%)
  starting transfers between devices  19.6 us (3%)
  between operations  18.3 us (3%)
    reduce_scatter x1, waiting for transfers between devices, on_device(): lax.psum_scatter(jnp.einsum('td,tsc->dsc', tokens, grad_mixed, preferred_...  160 us
    another operation x130, local copies, waits for them, and re-layouts, tap_sums(): return jnp.stack(pieces, 0)  69.8 us
    all_gather x1, waiting for transfers between devices, on_device(): gathered = lax.all_gather(w_in, 'ctx', axis=0, tiled=True)  57.9 us
    another operation x4, other arithmetic, on_device(): jnp.stack([first_grad, grad_product * filtered[:, 2], grad_product * filt...  47.7 us
    reduce_sum x17, other arithmetic, tap_sums(): pieces.append(jnp.sum(grads * ext[first:first + count] * keep_mask, axis=0))  44.6 us
    all_to_all x1, waiting for transfers between devices, on_device(): lax.all_to_all(loaded, 'ctx', split_axis=1, concat_axis=0, tiled=True)  32 us
    psum x1, waiting for transfers between devices, on_device(): lax.psum(long_local.astype(jnp.bfloat16), 'ctx').astype(jnp.float32)  31.4 us
    psum x1, blocking collectives, on_device(): lax.psum(jnp.transpose(short_local, (1, 0, 2)).astype(jnp.bfloat16), 'ctx')  23.7 us
  transfers between devices with their start and end apart: 12, of which 9 were waited for; matrix products, arithmetic and copies ran while one was open for 31% of the time, Pallas kernels for 0%

profile of v1, /device:TPU:0, one launch (start us, length us, event | category | flops | bytes accessed | tf_op | source)
XLA Modules:
  0.0 634.5 jit_solution(11685855656220909723)
XLA Ops:
  7.9 5.3 all-to-all-start
  21.6 32.0 %all-to-all-done = bf16[1,8,128,1024]{3,2,0,1:T(8,128)(2,1)S(1)} async-done(((bf16[1,8,128,1024]{3,2,0,1:T(8,128)(2,1)}), bf16[1,8,128,1024]{3,2,0,1:T(8,128)(2,1)S(1)}, u32[]{:S(2)}, u32[]{:S(2)}) %all-to-all-start) | async-done | bytes 2097184 | tf_op jit(solution)/shard_map/all_to_all | solution.py:59
  57.4 9.1 %collective-permute-done = bf16[256,1024]{1,0:T(8,128)(2,1)S(1)} collective-permute-done((bf16[256,1024]{1,0:T(8,128)(2,1)S(1)}, bf16[256,1024]{1,0:T(8,128)(2,1)S(1)}, u32[]{:S(2)}, u32[]{:S(2)}) %collective-permute-start) | collective-permute-done | bytes 524320 | tf_op jit(solution)/shard_map/ppermute | solution.py:75
  69.0 3.2 collective-permute-start.2
  72.3 10.9 %collective-permute-done.1 = bf16[256,1024]{1,0:T(8,128)(2,1)S(1)} collective-permute-done((bf16[256,1024]{1,0:T(8,128)(2,1)S(1)}, bf16[256,1024]{1,0:T(8,128)(2,1)S(1)}, u32[]{:S(2)}, u32[]{:S(2)}) %collective-permute-start.1) | collective-permute-done | bytes 524320 | tf_op jit(solution)/shard_map/ppermute | solution.py:75
  85.9 3.1 collective-permute-done.2
  93.3 57.9 %all-gather.2.cloned.1.call-done = bf16[4096,3,1024]{2,0,1:T(8,128)(2,1)} async-done(((bf16[512,3,1024]{2,0,1:T(8,128)(2,1)}), bf16[4096,3,1024]{2,0,1:T(8,128)(2,1)}) %all-gather.2.cloned.1.call-update) | async-done | bytes 25165840 | tf_op jit(solution)/shard_map/all_gather | solution.py:80
  151.2 12.2 %fusion.34 = bf16[256,3,1024]{2,0,1:T(8,128)(2,1)S(1)} fusion(bf16[4096,3,1024]{2,0,1:T(8,128)(2,1)} %all-gather.2.cloned.1.call-done, bf16[256,8192]{1,0:T(8,128)(2,1)} %constant_dynamic-update-slice_fusion, s32[]{:T(128)S(6)} %select_n.26), kind=kOutput, calls=%fused_computation.179 | convolution fusion | flops 6443237376 | bytes 28835844 | tf_op jit(solution)/shard_map/td,dsc->tsc/dot_general | solution.py:81
  167.0 3.6 multiply_add_fusion
  170.9 3.7 collective-permute-start.4
  176.3 2.7 fusion.268
  184.2 2.7 fusion.272
  187.1 2.7 fusion.274
  198.1 2.7 fusion.282
  203.7 2.6 fusion.286
  209.2 2.9 fusion.290
  212.4 3.3 fusion.292
  216.1 8.5 %multiply_add_fusion.2 = f32[256,1024]{1,0:T(8,128)S(1)} fusion(f32[383,1024]{1,0:T(8,128)S(1)} %maximum_convert_fusion.2, f32[256]{0:T(256)} %copy-done.108, f32[1024]{0:T(1024)S(1)} %bitcast.308, f32[256]{0:T(256)S(1)} %copy-done.109, f32[1024]{0:T(1024)S(1)} %bitcast.311, f32[256]{0:T(256)S(1)} %copy-done.110, f32[1024]{0:T(1024)S(1)} %bitcast.313, ...), kind=kLoop, calls=%fused_computation.834 | loop fusion | flops 33554432 | bytes 46357504 | tf_op jit(solution)/shard_map/add | solution.py:28
  224.6 19.1 %fusion.552 = (bf16[256,1,1024]{2,0,1:T(8,128)(2,1)}, f32[256,1024]{1,0:T(8,128)}) fusion(bf16[256,1024]{1,0:T(8,128)(2,1)} %param.13, f32[256]{0:T(256)} %get-tuple-element.435, f32[383,1024]{1,0:T(8,128)S(1)} %maximum_convert_fusion.2, f32[1024]{0:T(1024)} %bitcast.278, f32[256]{0:T(256)} %get-tuple-element.436, f32[1024]{0:T(1024)} %bitcast.280, ...), kind=kLoop, calls=%fused_computation.842 | loop fusion | flops 67633152 | bytes 92709888 | tf_op jit(solution)/shard_map/stack | solution.py:105
  244.0 3.2 fusion.294
  248.8 8.4 %fusion.488 = f32[256,1024]{1,0:T(8,128)} fusion(f32[383,1024]{1,0:T(8,128)S(1)} %maximum_convert_fusion.3, f32[256]{0:T(256)} %get-tuple-element.407, f32[256]{0:T(256)} %get-tuple-element.408, f32[256]{0:T(256)} %get-tuple-element.409, f32[256]{0:T(256)} %get-tuple-element.410, f32[256]{0:T(256)} %get-tuple-element.411, f32[256]{0:T(256)} %get-tuple-element.412, ...), kind=kLoop, calls=%fused_computation.734 | loop fusion | flops 24903680 | bytes 34766848 | tf_op jit(solution)/shard_map/add | solution.py:43
  257.3 25.0 %fusion.550 = (bf16[256,1,1024]{2,0,1:T(8,128)(2,1)}, f32[256,1024]{1,0:T(8,128)}) fusion(f32[256,3,1024]{2,0,1:T(8,128)} %copy-done.4, f32[256]{0:T(256)} %get-tuple-element.307, f32[383,1024]{1,0:T(8,128)S(1)} %maximum_convert_fusion.3, f32[1024]{0:T(1024)S(1)} %bitcast.279, f32[256]{0:T(256)} %get-tuple-element.308, f32[1024]{0:T(1024)S(1)} %bitcast.281, ...), kind=kLoop, calls=%fused_computation.840 | loop fusion | flops 76021760 | bytes 104824832 | tf_op jit(solution)/shard_map/stack | solution.py:105
  282.4 3.4 fusion.551
  348.0 10.6 %stack.704 = bf16[128,1024]{1,0:T(8,128)(2,1)} concatenate(bf16[1,1024]{1,0:T(2,128)(2,1)S(1)} %stack.576, bf16[1,1024]{1,0:T(2,128)(2,1)S(1)} %stack.577, bf16[1,1024]{1,0:T(2,128)(2,1)S(1)} %stack.578, bf16[1,1024]{1,0:T(2,128)(2,1)S(1)} %stack.579, bf16[1,1024]{1,0:T(2,128)(2,1)S(1)} %stack.580, bf16[1,1024]{1,0:T(2,128)(2,1)S(1)} %stack.581, bf16[1,1024]{1,0:T(2,128)(2,1)S(1)} %stack.582, ...), dimensions={0} | concatenate | bytes 524288 | tf_op jit(solution)/shard_map/stack | solution.py:55
  359.2 3.9 fusion.17
  363.1 13.2 %fusion = bf16[256,4096]{1,0:T(8,128)(2,1)} fusion(bf16[256,3,1024]{2,0,1:T(8,128)(2,1)S(1)} %fusion.17, bf16[4096,3,1024]{2,0,1:T(8,128)(2,1)} %all-gather.2.cloned.1.call-done), kind=kOutput, calls=%fused_computation.137 | convolution fusion | flops 6443499520 | bytes 28835840 | tf_op jit(solution)/shard_map/tsc,dsc->td/dot_general | solution.py:136
  376.3 13.5 %convolution_convert_fusion = bf16[4096,3,1024]{2,0,1:T(8,128)(2,1)} fusion(bf16[256,3,1024]{2,0,1:T(8,128)(2,1)S(1)} %fusion.17, bf16[256,8192]{1,0:T(8,128)(2,1)} %constant_dynamic-update-slice_fusion, s32[]{:T(128)S(6)} %select_n.26), kind=kOutput, calls=%fused_computation.128 | convolution fusion | flops 6455033856 | bytes 28835844 | tf_op jit(solution)/shard_map/td,tsc->dsc/dot_general | solution.py:143
  389.8 31.4 %all-reduce.2.cloned.1.call-done = bf16[128,1024]{1,0:T(8,128)(2,1)} async-done(((bf16[128,1024]{1,0:T(8,128)(2,1)}), bf16[128,1024]{1,0:T(8,128)(2,1)}) %all-reduce.2.cloned.1.call-update) | async-done | bytes 262160 | tf_op jit(solution)/shard_map/psum | solution.py:134
  425.3 3.7 fusion.14
  429.2 23.7 %psum.14 = bf16[3,7,1024]{2,0,1:T(4,128)(2,1)S(1)} all-reduce(bf16[3,7,1024]{2,0,1:T(4,128)(2,1)S(1)} %bitcast.213), channel_id=1, replica_groups=mesh['ctx'=8,'fsdp'=4] {'ctx'}, use_global_device_ids=true, to_apply=%region_13.14 | all-reduce | flops 21504 | bytes 86016 | tf_op jit(solution)/shard_map/psum | solution.py:131
  453.5 14.0 %reduce-scatter.3.cloned.1.call-done = bf16[256,1024]{1,0:T(8,128)(2,1)} async-done(((bf16[256,4096]{1,0:T(8,128)(2,1)}), bf16[256,1024]{1,0:T(8,128)(2,1)}) %reduce-scatter.3.cloned.1.call-update) | async-done | bytes 524304 | tf_op jit(solution)/shard_map/reduce_scatter | solution.py:139
  467.5 160.3 %reduce-scatter.5.cloned.1.call-done = bf16[512,3,1024]{2,0,1:T(8,128)(2,1)} async-done(((bf16[4096,3,1024]{2,0,1:T(8,128)(2,1)}), bf16[512,3,1024]{2,0,1:T(8,128)(2,1)}) %reduce-scatter.5.cloned.1.call-update) | async-done | bytes 3145744 | tf_op jit(solution)/shard_map/reduce_scatter | solution.py:142
  (739 shorter events, 113.8 us)
Async XLA Ops:
  7.2 144.0 %all-gather.2.cloned.1.call-start = ((), (), s32[]{:S(2)}) async-start(), calls=%async_computation.3 | async-start | bytes 28311552 | tf_op jit(solution)/shard_map/all_gather | solution.py:80
  7.9 45.7 %all-to-all-start = ((bf16[1,8,128,1024]{3,2,0,1:T(8,128)(2,1)}), bf16[1,8,128,1024]{3,2,0,1:T(8,128)(2,1)S(1)}, u32[]{:S(2)}, u32[]{:S(2)}) async-start(bf16[1,8,128,1024]{3,2,0,1:T(8,128)(2,1)} %bitcast.2), calls=%async_computation | async-start | bytes 4194304 | tf_op jit(solution)/shard_map/all_to_all | solution.py:59
  13.3 408.0 %all-reduce.2.cloned.1.call-start = ((), (), s32[]{:S(2)}) async-start(), calls=%async_computation.6 | async-start | bytes 524288 | tf_op jit(solution)/shard_map/psum | solution.py:134
  54.4 12.2 %collective-permute-start = (bf16[256,1024]{1,0:T(8,128)(2,1)S(1)}, bf16[256,1024]{1,0:T(8,128)(2,1)S(1)}, u32[]{:S(2)}, u32[]{:S(2)}) collective-permute-start(bf16[256,1024]{1,0:T(8,128)(2,1)S(1)} %convolution_convert_fusion.1), channel_id=1, source_target_pairs={{0,1},{1,2},{2,3},{3,0},{4,5},{5,6},{6,7},{7,4},{8,9},{9,10},{10,1... | collective-permute-start | bytes 1572872 | tf_op jit(solution)/shard_map/ppermute | solution.py:75
  66.6 16.7 %collective-permute-start.1 = (bf16[256,1024]{1,0:T(8,128)(2,1)S(1)}, bf16[256,1024]{1,0:T(8,128)(2,1)S(1)}, u32[]{:S(2)}, u32[]{:S(2)}) collective-permute-start(bf16[256,1024]{1,0:T(8,128)(2,1)S(1)} %collective-permute-done), channel_id=1, source_target_pairs={{0,1},{1,2},{2,3},{3,0},{4,5},{5,6},{6,7},{7,4},{8,9},{9,10},{10,1... | collective-permute-start | bytes 1572872 | tf_op jit(solution)/shard_map/ppermute | solution.py:75
  68.8 98.2 %copy-start.89 = (f32[256]{0:T(256)}, f32[256]{0:T(256)S(1)}, u32[]{:S(2)}) copy-start(f32[256]{0:T(256)S(1)} %get-tuple-element.555) | copy-start | bytes 3076
  68.8 98.2 %copy-start.92 = (f32[256]{0:T(256)}, f32[256]{0:T(256)S(1)}, u32[]{:S(2)}) copy-start(f32[256]{0:T(256)S(1)} %get-tuple-element.556) | copy-start | bytes 3076
  68.8 98.2 %copy-start.95 = (f32[256]{0:T(256)}, f32[256]{0:T(256)S(1)}, u32[]{:S(2)}) copy-start(f32[256]{0:T(256)S(1)} %get-tuple-element.557) | copy-start | bytes 3076
  68.8 98.2 %copy-start.98 = (f32[256]{0:T(256)}, f32[256]{0:T(256)S(1)}, u32[]{:S(2)}) copy-start(f32[256]{0:T(256)S(1)} %get-tuple-element.558) | copy-start | bytes 3076
  68.8 98.2 %copy-start.101 = (f32[256]{0:T(256)}, f32[256]{0:T(256)S(1)}, u32[]{:S(2)}) copy-start(f32[256]{0:T(256)S(1)} %get-tuple-element.559) | copy-start | bytes 3076
  68.8 98.2 %copy-start.104 = (f32[256]{0:T(256)}, f32[256]{0:T(256)S(1)}, u32[]{:S(2)}) copy-start(f32[256]{0:T(256)S(1)} %get-tuple-element.560) | copy-start | bytes 3076
  68.8 98.2 %copy-start.106 = (f32[256]{0:T(256)}, f32[256]{0:T(256)S(1)}, u32[]{:S(2)}) copy-start(f32[256]{0:T(256)S(1)} %get-tuple-element.561) | copy-start | bytes 3076
  68.9 107.3 %copy-start.147 = (f32[256]{0:T(256)}, f32[256]{0:T(256)S(1)}, u32[]{:S(2)}) copy-start(f32[256]{0:T(256)S(1)} %get-tuple-element.448) | copy-start | bytes 3076
  68.9 107.3 %copy-start.148 = (f32[256]{0:T(256)}, f32[256]{0:T(256)S(1)}, u32[]{:S(2)}) copy-start(f32[256]{0:T(256)S(1)} %get-tuple-element.450) | copy-start | bytes 3076
  68.9 107.3 %copy-start.149 = (f32[256]{0:T(256)}, f32[256]{0:T(256)S(1)}, u32[]{:S(2)}) copy-start(f32[256]{0:T(256)S(1)} %get-tuple-element.451) | copy-start | bytes 3076
  68.9 107.3 %copy-start.150 = (f32[256]{0:T(256)}, f32[256]{0:T(256)S(1)}, u32[]{:S(2)}) copy-start(f32[256]{0:T(256)S(1)} %get-tuple-element.452) | copy-start | bytes 3076
  68.9 107.3 %copy-start.151 = (f32[256]{0:T(256)}, f32[256]{0:T(256)S(1)}, u32[]{:S(2)}) copy-start(f32[256]{0:T(256)S(1)} %get-tuple-element.453) | copy-start | bytes 3076
  68.9 107.3 %copy-start.152 = (f32[256]{0:T(256)}, f32[256]{0:T(256)S(1)}, u32[]{:S(2)}) copy-start(f32[256]{0:T(256)S(1)} %get-tuple-element.454) | copy-start | bytes 3076
  68.9 107.3 %copy-start.153 = (f32[256]{0:T(256)}, f32[256]{0:T(256)S(1)}, u32[]{:S(2)}) copy-start(f32[256]{0:T(256)S(1)} %get-tuple-element.455) | copy-start | bytes 3076
  68.9 107.3 %copy-start.154 = (f32[256]{0:T(256)}, f32[256]{0:T(256)S(1)}, u32[]{:S(2)}) copy-start(f32[256]{0:T(256)S(1)} %get-tuple-element.456) | copy-start | bytes 3076
  68.9 107.3 %copy-start.155 = (f32[256]{0:T(256)}, f32[256]{0:T(256)S(1)}, u32[]{:S(2)}) copy-start(f32[256]{0:T(256)S(1)} %get-tuple-element.457) | copy-start | bytes 3076
  68.9 131.8 %copy-start.108 = (f32[256]{0:T(256)}, f32[256]{0:T(256)S(1)}, u32[]{:S(2)}) copy-start(f32[256]{0:T(256)S(1)} %get-tuple-element.519) | copy-start | bytes 3076
  69.0 20.0 %collective-permute-start.2 = (bf16[256,1024]{1,0:T(8,128)(2,1)S(1)}, bf16[256,1024]{1,0:T(8,128)(2,1)S(1)}, u32[]{:S(2)}, u32[]{:S(2)}) collective-permute-start(bf16[256,1024]{1,0:T(8,128)(2,1)S(1)} %convolution_convert_fusion.1), channel_id=1, source_target_pairs={{0,3},{1,0},{2,1},{3,2},{4,7},{5,4},{6,5},{7,6},{8,11},{9,8},{10,9... | collective-permute-start | bytes 1572872 | tf_op jit(solution)/shard_map/ppermute | solution.py:77
  163.4 3.0 collective-permute-start.3
  170.9 5.0 collective-permute-start.4
  179.0 64.7 %copy-start.2 = (bf16[256,1024]{1,0:T(8,128)(2,1)}, bf16[256,1024]{1,0:T(8,128)(2,1)S(1)}, u32[]{:S(2)}) copy-start(bf16[256,1024]{1,0:T(8,128)(2,1)S(1)} %get-tuple-element.154) | copy-start | bytes 1572868
  179.8 67.4 %collective-permute-start.5 = (bf16[127,1024]{1,0:T(8,128)(2,1)}, bf16[127,1024]{1,0:T(8,128)(2,1)S(1)}, u32[]{:S(2)}, u32[]{:S(2)}) collective-permute-start(bf16[127,1024]{1,0:T(8,128)(2,1)} %slice.2608), channel_id=1, source_target_pairs={{4,0},{8,4},{12,8},{16,12},{20,16},{24,20},{28,24},{5,1},{9,5},{13... | collective-permute-start | bytes 780296 | tf_op jit(solution)/shard_map/ppermute | solution.py:10
  285.8 73.0 %copy-start.9 = (bf16[256,1,1024]{2,0,1:T(8,128)(2,1)}, bf16[256,1,1024]{2,0,1:T(8,128)(2,1)S(1)}, u32[]{:S(2)}) copy-start(bf16[256,1,1024]{2,0,1:T(8,128)(2,1)S(1)} %get-tuple-element.162) | copy-start | bytes 1572868
  286.1 56.0 %copy-start.217 = (bf16[1024]{0:T(1024)(128)(2,1)S(1)}, bf16[1024]{0:T(1024)(128)(2,1)}, u32[]{:S(2)}) copy-start(bf16[1024]{0:T(1024)(128)(2,1)} %get-tuple-element.43) | copy-start | bytes 6148
  286.3 72.4 %collective-permute-start.6 = (bf16[6,3,1024]{2,0,1:T(8,128)(2,1)S(1)}, bf16[6,3,1024]{2,0,1:T(8,128)(2,1)S(1)}, u32[]{:S(2)}, u32[]{:S(2)}) collective-permute-start(bf16[6,3,1024]{2,0,1:T(8,128)(2,1)S(1)} %slice.2737), channel_id=1, source_target_pairs={{4,0},{8,4},{12,8},{16,12},{20,16},{24,20},{28,24},{5,1},{9,5},{13... | collective-permute-start | bytes 110600 | tf_op jit(solution)/shard_map/ppermute | solution.py:10
  358.7 108.8 %reduce-scatter.3.cloned.1.call-start = ((), (), s32[]{:S(2)}) async-start(), calls=%async_computation.4 | async-start | bytes 2621440 | tf_op jit(solution)/shard_map/reduce_scatter | solution.py:139
  376.2 251.5 %reduce-scatter.5.cloned.1.call-start = ((), (), s32[]{:S(2)}) async-start(), calls=%async_computation.5 | async-start | bytes 28311552 | tf_op jit(solution)/shard_map/reduce_scatter | solution.py:142
  (243 other events, 3189.8 us)
Sparse Core Ops, SparseCore 0:
  9.9 141.2 all-gather.1
  358.8 62.3 all-reduce.1
  424.2 43.2 reduce-scatter.2
  471.5 156.1 reduce-scatter.4
